TPU v7x, 32 devices: a whole 2x2x4 slice. The times are simulated.
32 devices in a mesh: mem: 4 (over x, core), lat: 8 (over z, y).
Axes of the slice: x: 2, y: 2, z: 4, core: 2. Of those that a mesh axis runs over, the one named last changes fastest.
Arguments:
- ensemble: float32 [256, 16, 512], P('mem', 'lat'), may hold values from -6 to 6
- diffusivity: float32 [16, 512], P('lat'), may hold values from 0.02 to 0.2
- north_wind: float32 [16, 512], P('lat'), may hold values from -0.25 to 0.25
- observed_blocks: int32 [8, 4, 4], P('lat'), may hold values from 0 to 7
- eastern_average_flags: int32 [8, 4, 512], P('lat'), may hold values 0 or 1
- observed_values: float32 [8, 4, 512], P('lat', 'mem'), may hold values from -6 to 6
- observed_error: float32 [8, 4, 512], P('lat', 'mem'), may hold values from 0.5 to 4
Outputs:
- analysis: float32 [256, 16, 512], P('mem', 'lat')
Inputs may be any that keep to these rules, and one draw needn't show every extreme that they name: `observed_blocks`: block i covers a band's flattened cells i * 128 to (i + 1) * 128 - 1; blocks may repeat.
All inputs are finite; a program needn't handle non-finite values. No bound on the sum of `eastern_average_flags` on one device may be relied on, other than what follows from the above.
Results may differ from a plain program's by a relative error of at most 0.0003.
Values sent between devices are 32-bit elements; how exact they have to be, the bound alone decides.
No kernel may reach another device: no remote copies, remote signals or barrier semaphores. Data moves between devices by JAX's collectives and lax.ppermute only.
A program may use at most 64 MiB of HBM per device.

v0:
```python
import jax
import jax.numpy as jnp
from jax import lax
from jax.sharding import PartitionSpec as P

OBS = 512
BLOCK = 128
NEWTON = 4
ADVECTION = 0.1
HIGHEST = lax.Precision.HIGHEST


def with_halo(block, sides, width):
    for axis, dim in sides:
        count = lax.axis_size(axis)
        forward = [(i, i + 1) for i in range(count - 1)]
        backward = [(target, source) for source, target in forward]
        low = lax.ppermute(
            lax.slice_in_dim(block, block.shape[dim] - width, None, axis=dim), axis, forward
        )
        high = lax.ppermute(lax.slice_in_dim(block, 0, width, axis=dim), axis, backward)
        block = jnp.concatenate([low, block, high], axis=dim)
    return block


def advance(padded, diffusivity, north_wind):
    centre = padded[:, 1:-1, :]
    northern = padded[:, :-2, :]
    equatorward_side = padded[:, 2:, :]
    eastern = jnp.roll(centre, -1, axis=2)
    western_neighbour = jnp.roll(centre, 1, axis=2)
    return (
        centre
        - ADVECTION * centre * (eastern - western_neighbour)
        - north_wind * (equatorward_side - northern)
        + diffusivity * (eastern + western_neighbour + northern + equatorward_side - 4.0 * centre)
    )


def contract_first(left, right):
    return lax.dot_general(
        left, right, (((0,), (0,)), ((), ())), precision=HIGHEST, preferred_element_type=jnp.float32
    )


def patch_gain(cell_values, seen_values, values, errors):
    sample_states = cell_values.shape[0]
    cell_offset = cell_values - jnp.mean(cell_values, axis=0)
    seen_mean = jnp.mean(seen_values, axis=0)
    seen_offset = seen_values - seen_mean
    covariance = contract_first(seen_offset, seen_offset) / (sample_states - 1.0) + jnp.diag(errors)
    row_scale = jnp.sum(jnp.abs(covariance), axis=1)
    inverse = jnp.diag(1.0 / row_scale)
    for sweep in range(NEWTON):
        product = jnp.dot(
            covariance, inverse, precision=HIGHEST, preferred_element_type=jnp.float32
        )
        inverse = 2.0 * inverse - jnp.dot(
            inverse, product, precision=HIGHEST, preferred_element_type=jnp.float32
        )
    cross_cov = contract_first(cell_offset, seen_offset) / (sample_states - 1.0)
    gain = jnp.dot(cross_cov, inverse, precision=HIGHEST, preferred_element_type=jnp.float32)
    innovation = values - seen_mean
    return (gain, innovation, seen_mean)


def body(
    ensemble,
    diffusivity,
    north_wind,
    observed_blocks,
    eastern_average_flags,
    observed_values,
    observed_error,
):
    local_members, row_count, meridian_total = ensemble.shape
    patch_count = lax.axis_size("mem")
    cell_count = row_count * meridian_total // patch_count
    coefficients = jnp.stack([diffusivity, north_wind])
    coef_rims = with_halo(coefficients, (("lat", 1),), 1)
    widened = with_halo(ensemble, (("lat", 1),), 2)
    variable_layers = advance(advance(widened, coef_rims[0], coef_rims[1]), diffusivity, north_wind)
    block_tiles = variable_layers.reshape(local_members, row_count * meridian_total // BLOCK, BLOCK)
    east_tiles = jnp.roll(variable_layers, -1, axis=2).reshape(
        local_members, row_count * meridian_total // BLOCK, BLOCK
    )
    chosen = observed_blocks[0].reshape(-1)
    direct = jnp.take(block_tiles, chosen, axis=1).reshape(local_members, patch_count, OBS)
    shifted = jnp.take(east_tiles, chosen, axis=1).reshape(local_members, patch_count, OBS)
    observed = jnp.where(eastern_average_flags[0][None] == 1, 0.5 * (direct + shifted), direct)
    owned = variable_layers.reshape(local_members, patch_count, cell_count)
    cell_values, seen_values = (
        lax.all_to_all(owned, "mem", split_axis=1, concat_axis=0, tiled=True),
        lax.all_to_all(observed, "mem", split_axis=1, concat_axis=0, tiled=True),
    )
    cell_values = cell_values[:, 0, :]
    seen_values = seen_values[:, 0, :]
    gain, innovation, seen_mean = patch_gain(
        cell_values, seen_values, observed_values[0, 0], observed_error[0, 0]
    )
    weights = innovation[None, :] - 0.5 * (seen_values - seen_mean[None, :])
    update = lax.dot_general(
        weights,
        gain,
        (((1,), (1,)), ((), ())),
        precision=HIGHEST,
        preferred_element_type=jnp.float32,
    )
    analysed = (cell_values + update)[:, None, :]
    returned = lax.all_to_all(analysed, "mem", split_axis=0, concat_axis=1, tiled=True)
    return returned.reshape(local_members, row_count, meridian_total)


def solution(mesh):
    return jax.shard_map(
        body,
        mesh=mesh,
        in_specs=(
            P("mem", "lat", None),
            P("lat", None),
            P("lat", None),
            P("lat", None, None),
            P("lat", None, None),
            P("lat", "mem", None),
            P("lat", "mem", None),
        ),
        out_specs=P("mem", "lat", None),
        check_vma=False,
    )
```

profile of v0, /device:TPU:0, one launch (start us, length us, event | category | flops | bytes accessed | tf_op | source)
XLA Modules:
  0.0 85.1 jit_solution(7209250416968997480)
XLA Ops:
  0.0 4.9 %collective-permute-start = (f32[64,2,512]{2,1,0:T(2,128)}, f32[64,2,512]{2,1,0:T(2,128)S(1)}, u32[]{:S(2)}, u32[]{:S(2)}) collective-permute-start(f32[64,2,512]{2,1,0:T(2,128)} %param.9), channel_id=1, source_target_pairs={{0,1},{1,2},{2,3},{3,4},{4,5},{5,6},{6,7},{8,9},{9,10},{10,11},{11... | collective-permute-start | bytes 786440 | tf_op jit(solution)/shard_map/ppermute | solution.py:18
  4.9 1.3 %collective-permute-start.1 = (f32[64,2,512]{2,1,0:T(2,128)}, f32[64,2,512]{2,1,0:T(2,128)S(1)}, u32[]{:S(2)}, u32[]{:S(2)}) collective-permute-start(f32[64,2,512]{2,1,0:T(2,128)} %param.9), channel_id=1, source_target_pairs={{1,0},{2,1},{3,2},{4,3},{5,4},{6,5},{7,6},{9,8},{10,9},{11,10},{12... | collective-permute-start | bytes 786440 | tf_op jit(solution)/shard_map/ppermute | solution.py:21
  6.2 0.8 fusion.25
  7.0 4.5 %collective-permute-start.2 = (f32[2,1,512]{2,1,0:T(1,128)S(1)}, f32[2,1,512]{2,1,0:T(1,128)S(1)}, u32[]{:S(2)}, u32[]{:S(2)}) collective-permute-start(f32[2,1,512]{2,1,0:T(1,128)S(1)} %get-tuple-element.14), channel_id=1, source_target_pairs={{0,1},{1,2},{2,3},{3,4},{4,5},{5,6},{6,7},{8,9},{9,10},{10,11},{11... | collective-permute-start | bytes 12296 | tf_op jit(solution)/shard_map/ppermute | solution.py:18
  11.6 1.3 %collective-permute-start.3 = (f32[2,1,512]{2,1,0:T(1,128)S(1)}, f32[2,1,512]{2,1,0:T(1,128)S(1)}, u32[]{:S(2)}, u32[]{:S(2)}) collective-permute-start(f32[2,1,512]{2,1,0:T(1,128)S(1)} %get-tuple-element.15), channel_id=1, source_target_pairs={{1,0},{2,1},{3,2},{4,3},{5,4},{6,5},{7,6},{9,8},{10,9},{11,10},{12... | collective-permute-start | bytes 12296 | tf_op jit(solution)/shard_map/ppermute | solution.py:21
  13.0 3.5 %collective-permute-done.2 = f32[2,1,512]{2,1,0:T(1,128)S(1)} collective-permute-done((f32[2,1,512]{2,1,0:T(1,128)S(1)}, f32[2,1,512]{2,1,0:T(1,128)S(1)}, u32[]{:S(2)}, u32[]{:S(2)}) %collective-permute-start.2) | collective-permute-done | bytes 4128 | tf_op jit(solution)/shard_map/ppermute | solution.py:18
  16.5 1.0 %collective-permute-done.3 = f32[2,1,512]{2,1,0:T(1,128)S(1)} collective-permute-done((f32[2,1,512]{2,1,0:T(1,128)S(1)}, f32[2,1,512]{2,1,0:T(1,128)S(1)}, u32[]{:S(2)}, u32[]{:S(2)}) %collective-permute-start.3) | collective-permute-done | bytes 4128 | tf_op jit(solution)/shard_map/ppermute | solution.py:21
  17.5 1.3 %pad_maximum_fusion = f32[64,6,512]{2,1,0:T(8,128)S(1)} fusion(f32[64,2,512]{2,1,0:T(2,128)S(1)} %collective-permute-done.1, f32[64,2,512]{2,1,0:T(2,128)} %param.9, f32[64,2,512]{2,1,0:T(2,128)S(1)} %collective-permute-done), kind=kLoop, calls=%fused_computation.18 | loop fusion | flops 393216 | bytes 1572864 | tf_op jit(solution)/shard_map/concatenate | solution.py:22
  19.8 1.3 %multiply_add_fusion = f32[64,4,512]{2,1,0:T(4,128)S(1)} fusion(f32[64,2,512]{2,1,0:T(2,128)S(1)} %copy-done, f32[64,2,512]{2,1,0:T(2,128)S(1)} %collective-permute-done, f32[64,2,512]{2,1,0:T(2,128)S(1)} %collective-permute-done.1, f32[64,4,511]{2,1,0:T(4,128)S(1)} %get-tuple-element.7, f32[64,4,511]{2,1,0:T(4,128)S(1)} %get-tuple-element.6, ...), kind=kLoop, calls=%fused_computation.42 | loop fusion | flops 2883584 | bytes 2897920 | tf_op jit(solution)/shard_map/add | solution.py:33
  21.7 0.9 %multiply_add_fusion.1 = f32[64,2,512]{2,1,0:T(2,128)S(1)} fusion(f32[64,4,512]{2,1,0:T(4,128)S(1)} %multiply_add_fusion, f32[64,2,511]{2,1,0:T(2,128)S(1)} %get-tuple-element.9, f32[64,2,1]{2,1,0:T(2,128)S(1)} %get-tuple-element.11, f32[64,2,1]{2,1,0:T(2,128)S(1)} %get-tuple-element.10, f32[64,2,511]{2,1,0:T(2,128)S(1)} %get-tuple-element.8, ...), kind=kLoop, calls=%fused_computation.50 | loop fusion | flops 1048576 | bytes 1581056 | tf_op jit(solution)/shard_map/add | solution.py:33
  26.3 0.8 copy.36
  27.0 3.4 %all-to-all-start = ((f32[64,4,256]{2,0,1:T(8,128)}), f32[64,4,256]{2,0,1:T(8,128)S(1)}, u32[]{:S(2)}, u32[]{:S(2)}) async-start(f32[64,4,256]{2,0,1:T(8,128)} %copy.36), calls=%async_computation | async-start | bytes 524288 | tf_op jit(solution)/shard_map/all_to_all | solution.py:93
  30.6 1.0 %copy.41 = f32[64,4,512]{2,0,1:T(8,128)} copy(f32[64,4,512]{2,1,0:T(4,128)S(1)} %multiply_select_fusion) | data formatting | bytes 1048576 | tf_op jit(solution)/shard_map/jit(_where)/select_n | solution.py:90
  31.6 4.8 %all-to-all-done = f32[64,4,256]{2,0,1:T(8,128)S(1)} async-done(((f32[64,4,256]{2,0,1:T(8,128)}), f32[64,4,256]{2,0,1:T(8,128)S(1)}, u32[]{:S(2)}, u32[]{:S(2)}) %all-to-all-start) | async-done | bytes 262176 | tf_op jit(solution)/shard_map/all_to_all | solution.py:93
  36.4 3.6 %all-to-all-start.1 = ((f32[64,4,512]{2,0,1:T(8,128)}), f32[64,4,512]{2,0,1:T(8,128)S(1)}, u32[]{:S(2)}, u32[]{:S(2)}) async-start(f32[64,4,512]{2,0,1:T(8,128)} %copy.41), calls=%async_computation.1 | async-start | bytes 1048576 | tf_op jit(solution)/shard_map/all_to_all | solution.py:94
  40.1 8.5 %all-to-all-done.1 = f32[64,4,512]{2,0,1:T(8,128)S(1)} async-done(((f32[64,4,512]{2,0,1:T(8,128)}), f32[64,4,512]{2,0,1:T(8,128)S(1)}, u32[]{:S(2)}, u32[]{:S(2)}) %all-to-all-start.1) | async-done | bytes 524320 | tf_op jit(solution)/shard_map/all_to_all | solution.py:94
  48.7 0.6 copy-done.5
  49.3 0.7 copy-done.6
  50.0 1.2 %abs_reduce_fusion = (f32[512]{0:T(512)S(1)}, f32[512,512]{0,1:T(8,128)S(1)}) fusion(f32[512]{0:T(512)S(1)} %bitcast.94, f32[64,4,512]{2,0,1:T(8,128)S(1)} %all-to-all-done.1, f32[512]{0:T(512)S(1)} %get-tuple-element.17), kind=kOutput, calls=%fused_computation.19 | convolution fusion | flops 807009792 | bytes 1579008 | tf_op jit(solution)/shard_map/dot_general | solution.py:41
  51.2 3.5 %fusion.2 = f32[512,512]{1,0:T(8,128)S(1)} fusion(f32[512,512]{0,1:T(8,128)S(1)} %get-tuple-element.21, f32[512]{0:T(512)S(1)} %broadcast_divide_fusion), kind=kOutput, calls=%fused_computation.4 | convolution fusion | flops 1611137024 | bytes 2099200 | tf_op jit(solution)/shard_map/dot_general | solution.py:55
  54.7 1.9 %fusion.4 = f32[512,512]{0,1:T(8,128)S(1)} fusion(f32[512,512]{1,0:T(8,128)S(1)} %fusion.2, f32[512]{0:T(512)S(1)} %broadcast_divide_fusion), kind=kOutput, calls=%fused_computation.7 | convolution fusion | flops 1612185600 | bytes 2099200 | tf_op jit(solution)/shard_map/dot_general | solution.py:58
  56.6 3.5 %fusion.32 = f32[512,512]{1,0:T(8,128)S(1)} fusion(f32[512,512]{0,1:T(8,128)S(1)} %get-tuple-element.21, f32[512,512]{0,1:T(8,128)S(1)} %fusion.4), kind=kOutput, calls=%fused_computation.72 | convolution fusion | flops 1610612736 | bytes 3145728 | tf_op jit(solution)/shard_map/dot_general | solution.py:55
  60.1 1.9 %convolution_subtract_fusion.2 = f32[512,512]{0,1:T(8,128)S(1)} fusion(f32[512,512]{0,1:T(8,128)S(1)} %fusion.4, f32[512,512]{1,0:T(8,128)S(1)} %fusion.32), kind=kOutput, calls=%fused_computation.10 | convolution fusion | flops 1611137024 | bytes 3145728 | tf_op jit(solution)/shard_map/dot_general | solution.py:58
  62.0 3.7 %fusion.33 = f32[512,512]{1,0:T(8,128)S(1)} fusion(f32[512,512]{0,1:T(8,128)S(1)} %get-tuple-element.21, f32[512,512]{0,1:T(8,128)S(1)} %convolution_subtract_fusion.2), kind=kOutput, calls=%fused_computation.73 | convolution fusion | flops 1610612736 | bytes 3145728 | tf_op jit(solution)/shard_map/dot_general | solution.py:55
  65.7 1.9 %convolution_subtract_fusion.1 = f32[512,512]{0,1:T(8,128)S(1)} fusion(f32[512,512]{0,1:T(8,128)S(1)} %convolution_subtract_fusion.2, f32[512,512]{1,0:T(8,128)S(1)} %fusion.33), kind=kOutput, calls=%fused_computation.9 | convolution fusion | flops 1611137024 | bytes 3145728 | tf_op jit(solution)/shard_map/dot_general | solution.py:58
  67.5 3.5 %fusion.34 = f32[512,512]{1,0:T(8,128)S(1)} fusion(f32[512,512]{0,1:T(8,128)S(1)} %get-tuple-element.21, f32[512,512]{0,1:T(8,128)S(1)} %convolution_subtract_fusion.1), kind=kOutput, calls=%fused_computation.74 | convolution fusion | flops 1610612736 | bytes 3145728 | tf_op jit(solution)/shard_map/dot_general | solution.py:55
  71.0 1.9 %convolution_subtract_fusion = f32[512,512]{0,1:T(8,128)S(1)} fusion(f32[512,512]{0,1:T(8,128)S(1)} %convolution_subtract_fusion.1, f32[512,512]{1,0:T(8,128)S(1)} %fusion.34), kind=kOutput, calls=%fused_computation.8 | convolution fusion | flops 1611137024 | bytes 3145728 | tf_op jit(solution)/shard_map/dot_general | solution.py:58
  72.9 0.7 fusion.9
  73.6 1.1 %fusion.35 = f32[256,512]{1,0:T(8,128)S(1)} fusion(f32[256,512]{1,0:T(8,128)S(1)} %fusion.9, f32[512,512]{0,1:T(8,128)S(1)} %convolution_subtract_fusion), kind=kOutput, calls=%fused_computation.75 | convolution fusion | flops 805306368 | bytes 2097152 | tf_op jit(solution)/shard_map/dot_general | solution.py:62
  74.7 0.6 fusion.10
  75.6 8.4 %all_to_all.45 = f32[256,1,256]{2,1,0:T(1,128)S(1)} all-to-all(f32[256,1,256]{2,1,0:T(1,128)S(1)} %copy.46), channel_id=1, replica_groups=mesh['mem'=4,'lat'=8] {'mem'}, dimensions={0} | all-to-all | bytes 524288 | tf_op jit(solution)/shard_map/all_to_all | solution.py:110
  84.2 0.9 %reshape.89 = f32[64,2,512]{2,1,0:T(2,128)} reshape(f32[64,4,1,256]{3,1,0,2:T(4,128)S(1)} %copy.47) | data formatting | bytes 524288 | tf_op jit(solution)/shard_map/reshape | solution.py:111
  (48 shorter events, 6.1 us)
Async XLA Ops:
  0.0 17.5 %collective-permute-start = (f32[64,2,512]{2,1,0:T(2,128)}, f32[64,2,512]{2,1,0:T(2,128)S(1)}, u32[]{:S(2)}, u32[]{:S(2)}) collective-permute-start(f32[64,2,512]{2,1,0:T(2,128)} %param.9), channel_id=1, source_target_pairs={{0,1},{1,2},{2,3},{3,4},{4,5},{5,6},{6,7},{8,9},{9,10},{10,11},{11... | collective-permute-start | bytes 786440 | tf_op jit(solution)/shard_map/ppermute | solution.py:18
  4.9 12.6 %collective-permute-start.1 = (f32[64,2,512]{2,1,0:T(2,128)}, f32[64,2,512]{2,1,0:T(2,128)S(1)}, u32[]{:S(2)}, u32[]{:S(2)}) collective-permute-start(f32[64,2,512]{2,1,0:T(2,128)} %param.9), channel_id=1, source_target_pairs={{1,0},{2,1},{3,2},{4,3},{5,4},{6,5},{7,6},{9,8},{10,9},{11,10},{12... | collective-permute-start | bytes 786440 | tf_op jit(solution)/shard_map/ppermute | solution.py:21
  6.2 6.7 %copy-start.4 = (s32[1,4,4]{2,1,0:T(4,128)S(1)}, s32[1,4,4]{2,1,0:T(4,128)}, u32[]{:S(2)}) copy-start(s32[1,4,4]{2,1,0:T(4,128)} %param.12) | copy-start | bytes 196
  7.0 6.0 %copy-start.3 = (s32[1,4,512]{2,1,0:T(4,128)S(1)}, s32[1,4,512]{2,1,0:T(4,128)}, u32[]{:S(2)}) copy-start(s32[1,4,512]{2,1,0:T(4,128)} %param.13) | copy-start | bytes 24580
  7.0 9.5 %collective-permute-start.2 = (f32[2,1,512]{2,1,0:T(1,128)S(1)}, f32[2,1,512]{2,1,0:T(1,128)S(1)}, u32[]{:S(2)}, u32[]{:S(2)}) collective-permute-start(f32[2,1,512]{2,1,0:T(1,128)S(1)} %get-tuple-element.14), channel_id=1, source_target_pairs={{0,1},{1,2},{2,3},{3,4},{4,5},{5,6},{6,7},{8,9},{9,10},{10,11},{11... | collective-permute-start | bytes 12296 | tf_op jit(solution)/shard_map/ppermute | solution.py:18
  11.6 5.9 %collective-permute-start.3 = (f32[2,1,512]{2,1,0:T(1,128)S(1)}, f32[2,1,512]{2,1,0:T(1,128)S(1)}, u32[]{:S(2)}, u32[]{:S(2)}) collective-permute-start(f32[2,1,512]{2,1,0:T(1,128)S(1)} %get-tuple-element.15), channel_id=1, source_target_pairs={{1,0},{2,1},{3,2},{4,3},{5,4},{6,5},{7,6},{9,8},{10,9},{11,10},{12... | collective-permute-start | bytes 12296 | tf_op jit(solution)/shard_map/ppermute | solution.py:21
  13.0 4.5 %copy-start.2 = (f32[2,512]{1,0:T(2,128)S(1)}, f32[2,512]{1,0:T(2,128)}, u32[]{:S(2)}) copy-start(f32[2,512]{1,0:T(2,128)} %param.11) | copy-start | bytes 12292
  13.0 4.5 %copy-start.1 = (f32[2,512]{1,0:T(2,128)S(1)}, f32[2,512]{1,0:T(2,128)}, u32[]{:S(2)}) copy-start(f32[2,512]{1,0:T(2,128)} %param.10) | copy-start | bytes 12292
  18.8 1.0 %copy-start = (f32[64,2,512]{2,1,0:T(2,128)S(1)}, f32[64,2,512]{2,1,0:T(2,128)}, u32[]{:S(2)}) copy-start(f32[64,2,512]{2,1,0:T(2,128)} %param.9) | copy-start | bytes 786436
  27.0 9.4 %all-to-all-start = ((f32[64,4,256]{2,0,1:T(8,128)}), f32[64,4,256]{2,0,1:T(8,128)S(1)}, u32[]{:S(2)}, u32[]{:S(2)}) async-start(f32[64,4,256]{2,0,1:T(8,128)} %copy.36), calls=%async_computation | async-start | bytes 524288 | tf_op jit(solution)/shard_map/all_to_all | solution.py:93
  36.4 12.3 %all-to-all-start.1 = ((f32[64,4,512]{2,0,1:T(8,128)}), f32[64,4,512]{2,0,1:T(8,128)S(1)}, u32[]{:S(2)}, u32[]{:S(2)}) async-start(f32[64,4,512]{2,0,1:T(8,128)} %copy.41), calls=%async_computation.1 | async-start | bytes 1048576 | tf_op jit(solution)/shard_map/all_to_all | solution.py:94
  48.7 0.7 copy-start.5
  49.3 0.7 copy-start.6
where the time goes:
time: 85.7 us; the launch traced here: 85.1 us
  matrix products  25.2 us (29%)
  starting transfers between devices  19.1 us (22%)
  waiting for transfers between devices  17.8 us (21%)
  local copies, waits for them, and re-layouts  9.31 us (11%)
  blocking collectives  8.39 us (10%)
  other arithmetic  4.96 us (6%)
    dot_general x4, matrix products, patch_gain(): jnp.dot(covariance, inverse, precision=HIGHEST, preferred_element_type=jn...  14.1 us
    ppermute x2, starting transfers between devices, with_halo(): lax.ppermute(lax.slice_in_dim(block, block.shape[dim] - width, None, axis...  9.45 us
    all_to_all x1, waiting for transfers between devices, body(): lax.all_to_all(observed, 'mem', split_axis=1, concat_axis=0, tiled=True)  8.54 us
    all_to_all x1, blocking collectives, body(): lax.all_to_all(analysed, 'mem', split_axis=0, concat_axis=1, tiled=True)  8.39 us
    dot_general x4, matrix products, patch_gain(): jnp.dot(inverse, product, precision=HIGHEST, preferred_element_type=jnp.f...  7.55 us
    all_to_all x1, waiting for transfers between devices, body(): lax.all_to_all(owned, 'mem', split_axis=1, concat_axis=0, tiled=True)  4.83 us
    all_to_all x1, starting transfers between devices, body(): lax.all_to_all(observed, 'mem', split_axis=1, concat_axis=0, tiled=True)  3.65 us
    ppermute x2, waiting for transfers between devices, with_halo(): lax.ppermute(lax.slice_in_dim(block, block.shape[dim] - width, None, axis...  3.46 us
  transfers between devices with their start and end apart: 6, of which 4 were waited for; matrix products, arithmetic and copies ran while one was open for 2% of the time, Pallas kernels for 0%

commit v1 on v0

--- a/solution.py
+++ b/solution.py
@@ -8,6 +8,22 @@
 NEWTON = 4
 ADVECTION = 0.1
 HIGHEST = lax.Precision.HIGHEST
+
+
+def exchange_in_pairs(x, axis, split, join):
+    ways, here = (lax.axis_size(axis), lax.axis_index(axis))
+    width = x.shape[split] // ways
+    shape = list(x.shape)
+    shape[split] = width
+    height = shape[join]
+    shape[join] = height * ways
+    full = jnp.zeros(shape, x.dtype)
+    for mask in range(ways):
+        part = lax.dynamic_slice_in_dim(x, (here ^ mask) * width, width, axis=split)
+        if mask:
+            part = lax.ppermute(part, axis, [(d, d ^ mask) for d in range(ways)])
+        full = lax.dynamic_update_slice_in_dim(full, part, (here ^ mask) * height, axis=join)
+    return full
 
 
 def with_halo(block, sides, width):
@@ -90,7 +106,7 @@
     observed = jnp.where(eastern_average_flags[0][None] == 1, 0.5 * (direct + shifted), direct)
     owned = variable_layers.reshape(local_members, patch_count, cell_count)
     cell_values, seen_values = (
-        lax.all_to_all(owned, "mem", split_axis=1, concat_axis=0, tiled=True),
+        exchange_in_pairs(owned, "mem", 1, 0),
         lax.all_to_all(observed, "mem", split_axis=1, concat_axis=0, tiled=True),
     )
     cell_values = cell_values[:, 0, :]

time: 85.7 us -> 78.9 us (0.921)
  waiting for transfers between devices: 17.8 us -> 12.8 us
  starting transfers between devices: 19.1 us -> 17.7 us
    all_to_all x1, waiting for transfers between devices: 8.54 us -> 0.01 us  [body(): lax.all_to_all(observed, 'mem', split_axis=1, concat_axis=0, tiled=True)]
    ppermute x0 -> x3, waiting for transfers between devices: none -> 8.42 us  [exchange_in_pairs(): part = lax.ppermute(part, axis, [(d, d ^ mask) for d in range(ways)])]
    all_to_all x1 -> x0, waiting for transfers between devices: 4.83 us -> none  [body(): lax.all_to_all(owned, 'mem', split_axis=1, concat_axis=0, tiled=True)]
    all_to_all x1 -> x0, starting transfers between devices: 3.41 us -> none  [body(): lax.all_to_all(owned, 'mem', split_axis=1, concat_axis=0, tiled=True)]
    ppermute x0 -> x3, starting transfers between devices: none -> 2.06 us  [exchange_in_pairs(): part = lax.ppermute(part, axis, [(d, d ^ mask) for d in range(ways)])]
    unnamed x14 -> x17, local copies, waits for them, and re-layouts: 1.82 us -> 1.83 us
  transfers between devices with their start and end apart: 6 -> 8, of which waited for: 4 -> 4; matrix products, arithmetic and copies ran while one was open for 2% -> 2% of each run, Pallas kernels for 0% -> 0%
where the time goes in v1:
time: 78.9 us; the launch traced here: 78.5 us
  matrix products  25.2 us (32%)
  starting transfers between devices  17.7 us (22%)
  waiting for transfers between devices  12.8 us (16%)
  local copies, waits for them, and re-layouts  8.86 us (11%)
  blocking collectives  8.39 us (11%)
  other arithmetic  4.96 us (6%)
    dot_general x4, matrix products, patch_gain(): jnp.dot(covariance, inverse, precision=HIGHEST, preferred_element_type=jn...  13.9 us
    ppermute x2, starting transfers between devices, with_halo(): lax.ppermute(lax.slice_in_dim(block, block.shape[dim] - width, None, axis...  9.45 us
    ppermute x3, waiting for transfers between devices, exchange_in_pairs(): part = lax.ppermute(part, axis, [(d, d ^ mask) for d in range(ways)])  8.42 us
    all_to_all x1, blocking collectives, body(): lax.all_to_all(analysed, 'mem', split_axis=0, concat_axis=1, tiled=True)  8.39 us
    dot_general x4, matrix products, patch_gain(): jnp.dot(inverse, product, precision=HIGHEST, preferred_element_type=jnp.f...  7.79 us
    all_to_all x1, starting transfers between devices, body(): lax.all_to_all(observed, 'mem', split_axis=1, concat_axis=0, tiled=True)  3.65 us
    ppermute x2, waiting for transfers between devices, with_halo(): lax.ppermute(lax.slice_in_dim(block, block.shape[dim] - width, None, axis...  3.42 us
    ppermute x2, starting transfers between devices, with_halo(): lax.ppermute(lax.slice_in_dim(block, 0, width, axis=dim), axis, backward)  2.58 us
  transfers between devices with their start and end apart: 8, of which 4 were waited for; matrix products, arithmetic and copies ran while one was open for 2% of the time, Pallas kernels for 0%

profile of v1, /device:TPU:0, one launch (start us, length us, event | category | flops | bytes accessed | tf_op | source)
XLA Modules:
  0.0 78.5 jit_solution(3109375871619051397)
XLA Ops:
  0.0 4.9 %collective-permute-start = (f32[64,2,512]{2,1,0:T(2,128)}, f32[64,2,512]{2,1,0:T(2,128)S(1)}, u32[]{:S(2)}, u32[]{:S(2)}) collective-permute-start(f32[64,2,512]{2,1,0:T(2,128)} %param.9), channel_id=1, source_target_pairs={{0,1},{1,2},{2,3},{3,4},{4,5},{5,6},{6,7},{8,9},{9,10},{10,11},{11... | collective-permute-start | bytes 786440 | tf_op jit(solution)/shard_map/ppermute | solution.py:34
  4.9 1.3 %collective-permute-start.1 = (f32[64,2,512]{2,1,0:T(2,128)}, f32[64,2,512]{2,1,0:T(2,128)S(1)}, u32[]{:S(2)}, u32[]{:S(2)}) collective-permute-start(f32[64,2,512]{2,1,0:T(2,128)} %param.9), channel_id=1, source_target_pairs={{1,0},{2,1},{3,2},{4,3},{5,4},{6,5},{7,6},{9,8},{10,9},{11,10},{12... | collective-permute-start | bytes 786440 | tf_op jit(solution)/shard_map/ppermute | solution.py:37
  6.2 0.8 fusion.24
  7.0 4.5 %collective-permute-start.2 = (f32[2,1,512]{2,1,0:T(1,128)S(1)}, f32[2,1,512]{2,1,0:T(1,128)S(1)}, u32[]{:S(2)}, u32[]{:S(2)}) collective-permute-start(f32[2,1,512]{2,1,0:T(1,128)S(1)} %get-tuple-element.18), channel_id=1, source_target_pairs={{0,1},{1,2},{2,3},{3,4},{4,5},{5,6},{6,7},{8,9},{9,10},{10,11},{11... | collective-permute-start | bytes 12296 | tf_op jit(solution)/shard_map/ppermute | solution.py:34
  11.6 1.3 %collective-permute-start.3 = (f32[2,1,512]{2,1,0:T(1,128)S(1)}, f32[2,1,512]{2,1,0:T(1,128)S(1)}, u32[]{:S(2)}, u32[]{:S(2)}) collective-permute-start(f32[2,1,512]{2,1,0:T(1,128)S(1)} %get-tuple-element.19), channel_id=1, source_target_pairs={{1,0},{2,1},{3,2},{4,3},{5,4},{6,5},{7,6},{9,8},{10,9},{11,10},{12... | collective-permute-start | bytes 12296 | tf_op jit(solution)/shard_map/ppermute | solution.py:37
  13.1 3.4 %collective-permute-done.2 = f32[2,1,512]{2,1,0:T(1,128)S(1)} collective-permute-done((f32[2,1,512]{2,1,0:T(1,128)S(1)}, f32[2,1,512]{2,1,0:T(1,128)S(1)}, u32[]{:S(2)}, u32[]{:S(2)}) %collective-permute-start.2) | collective-permute-done | bytes 4128 | tf_op jit(solution)/shard_map/ppermute | solution.py:34
  16.5 1.0 %collective-permute-done.3 = f32[2,1,512]{2,1,0:T(1,128)S(1)} collective-permute-done((f32[2,1,512]{2,1,0:T(1,128)S(1)}, f32[2,1,512]{2,1,0:T(1,128)S(1)}, u32[]{:S(2)}, u32[]{:S(2)}) %collective-permute-start.3) | collective-permute-done | bytes 4128 | tf_op jit(solution)/shard_map/ppermute | solution.py:37
  17.5 1.3 %pad_maximum_fusion = f32[64,6,512]{2,1,0:T(8,128)S(1)} fusion(f32[64,2,512]{2,1,0:T(2,128)S(1)} %collective-permute-done.1, f32[64,2,512]{2,1,0:T(2,128)} %param.9, f32[64,2,512]{2,1,0:T(2,128)S(1)} %collective-permute-done), kind=kLoop, calls=%fused_computation.17 | loop fusion | flops 393216 | bytes 1572864 | tf_op jit(solution)/shard_map/concatenate | solution.py:38
  19.8 1.3 %multiply_add_fusion = f32[64,4,512]{2,1,0:T(4,128)S(1)} fusion(f32[64,2,512]{2,1,0:T(2,128)S(1)} %copy-done, f32[64,2,512]{2,1,0:T(2,128)S(1)} %collective-permute-done, f32[64,2,512]{2,1,0:T(2,128)S(1)} %collective-permute-done.1, f32[64,4,511]{2,1,0:T(4,128)S(1)} %get-tuple-element.7, f32[64,4,511]{2,1,0:T(4,128)S(1)} %get-tuple-element.6, ...), kind=kLoop, calls=%fused_computation.40 | loop fusion | flops 2883584 | bytes 2897920 | tf_op jit(solution)/shard_map/add | solution.py:49
  21.7 0.9 %multiply_add_fusion.1 = f32[64,2,512]{2,1,0:T(2,128)S(1)} fusion(f32[64,4,512]{2,1,0:T(4,128)S(1)} %multiply_add_fusion, f32[64,2,511]{2,1,0:T(2,128)S(1)} %get-tuple-element.9, f32[64,2,1]{2,1,0:T(2,128)S(1)} %get-tuple-element.11, f32[64,2,1]{2,1,0:T(2,128)S(1)} %get-tuple-element.10, f32[64,2,511]{2,1,0:T(2,128)S(1)} %get-tuple-element.8, ...), kind=kLoop, calls=%fused_computation.48 | loop fusion | flops 1048576 | bytes 1581056 | tf_op jit(solution)/shard_map/add | solution.py:49
  23.9 0.6 gather_fusion.1
  24.5 0.6 gather_fusion
  26.4 1.0 %copy.45 = f32[64,4,512]{2,0,1:T(8,128)} copy(f32[64,4,512]{2,1,0:T(4,128)S(1)} %multiply_select_fusion) | data formatting | bytes 1048576 | tf_op jit(solution)/shard_map/jit(_where)/select_n | solution.py:106
  27.4 3.6 %all-to-all-start = ((f32[64,4,512]{2,0,1:T(8,128)}), f32[64,4,512]{2,0,1:T(8,128)S(1)}, u32[]{:S(2)}, u32[]{:S(2)}) async-start(f32[64,4,512]{2,0,1:T(8,128)} %copy.45), calls=%async_computation | async-start | bytes 1048576 | tf_op jit(solution)/shard_map/all_to_all | solution.py:110
  31.7 1.6 %collective-permute-start.5 = (f32[64,1,256]{2,0,1:T(8,128)S(1)}, f32[64,1,256]{2,0,1:T(8,128)S(1)}, u32[]{:S(2)}, u32[]{:S(2)}) collective-permute-start(f32[64,1,256]{2,0,1:T(8,128)S(1)} %copy.58), channel_id=1, source_target_pairs={{0,16},{8,24},{16,0},{24,8},{1,17},{9,25},{17,1},{25,9},{2,18},{10... | collective-permute-start | bytes 196616 | tf_op jit(solution)/shard_map/ppermute | solution.py:24
  33.5 8.2 %collective-permute-done.5 = f32[64,1,256]{2,0,1:T(8,128)S(1)} collective-permute-done((f32[64,1,256]{2,0,1:T(8,128)S(1)}, f32[64,1,256]{2,0,1:T(8,128)S(1)}, u32[]{:S(2)}, u32[]{:S(2)}) %collective-permute-start.5) | collective-permute-done | bytes 65568 | tf_op jit(solution)/shard_map/ppermute | solution.py:24
  42.0 0.6 copy-done.5
  42.7 0.7 copy-done.6
  43.3 1.2 %abs_reduce_fusion = (f32[512]{0:T(512)S(1)}, f32[512,512]{0,1:T(8,128)S(1)}) fusion(f32[512]{0:T(512)S(1)} %bitcast.76, f32[64,4,512]{2,0,1:T(8,128)S(1)} %all-to-all-done, f32[512]{0:T(512)S(1)} %get-tuple-element.21), kind=kOutput, calls=%fused_computation.18 | convolution fusion | flops 807009792 | bytes 1579008 | tf_op jit(solution)/shard_map/dot_general | solution.py:57
  44.5 3.5 %fusion.2 = f32[512,512]{1,0:T(8,128)S(1)} fusion(f32[512,512]{0,1:T(8,128)S(1)} %get-tuple-element.25, f32[512]{0:T(512)S(1)} %broadcast_divide_fusion), kind=kOutput, calls=%fused_computation.4 | convolution fusion | flops 1611137024 | bytes 2099200 | tf_op jit(solution)/shard_map/dot_general | solution.py:71
  48.0 1.9 %fusion.4 = f32[512,512]{0,1:T(8,128)S(1)} fusion(f32[512,512]{1,0:T(8,128)S(1)} %fusion.2, f32[512]{0:T(512)S(1)} %broadcast_divide_fusion), kind=kOutput, calls=%fused_computation.7 | convolution fusion | flops 1612185600 | bytes 2099200 | tf_op jit(solution)/shard_map/dot_general | solution.py:74
  49.9 3.5 %fusion.32 = f32[512,512]{1,0:T(8,128)S(1)} fusion(f32[512,512]{0,1:T(8,128)S(1)} %get-tuple-element.25, f32[512,512]{0,1:T(8,128)S(1)} %fusion.4), kind=kOutput, calls=%fused_computation.79 | convolution fusion | flops 1610612736 | bytes 3145728 | tf_op jit(solution)/shard_map/dot_general | solution.py:71
  53.4 2.1 %convolution_subtract_fusion.2 = f32[512,512]{0,1:T(8,128)S(1)} fusion(f32[512,512]{0,1:T(8,128)S(1)} %fusion.4, f32[512,512]{1,0:T(8,128)S(1)} %fusion.32), kind=kOutput, calls=%fused_computation.10 | convolution fusion | flops 1611137024 | bytes 3145728 | tf_op jit(solution)/shard_map/dot_general | solution.py:74
  55.5 3.5 %fusion.33 = f32[512,512]{1,0:T(8,128)S(1)} fusion(f32[512,512]{0,1:T(8,128)S(1)} %get-tuple-element.25, f32[512,512]{0,1:T(8,128)S(1)} %convolution_subtract_fusion.2), kind=kOutput, calls=%fused_computation.80 | convolution fusion | flops 1610612736 | bytes 3145728 | tf_op jit(solution)/shard_map/dot_general | solution.py:71
  59.0 1.9 %convolution_subtract_fusion.1 = f32[512,512]{0,1:T(8,128)S(1)} fusion(f32[512,512]{0,1:T(8,128)S(1)} %convolution_subtract_fusion.2, f32[512,512]{1,0:T(8,128)S(1)} %fusion.33), kind=kOutput, calls=%fused_computation.9 | convolution fusion | flops 1611137024 | bytes 3145728 | tf_op jit(solution)/shard_map/dot_general | solution.py:74
  60.9 3.5 %fusion.34 = f32[512,512]{1,0:T(8,128)S(1)} fusion(f32[512,512]{0,1:T(8,128)S(1)} %get-tuple-element.25, f32[512,512]{0,1:T(8,128)S(1)} %convolution_subtract_fusion.1), kind=kOutput, calls=%fused_computation.81 | convolution fusion | flops 1610612736 | bytes 3145728 | tf_op jit(solution)/shard_map/dot_general | solution.py:71
  64.4 1.9 %convolution_subtract_fusion = f32[512,512]{0,1:T(8,128)S(1)} fusion(f32[512,512]{0,1:T(8,128)S(1)} %convolution_subtract_fusion.1, f32[512,512]{1,0:T(8,128)S(1)} %fusion.34), kind=kOutput, calls=%fused_computation.8 | convolution fusion | flops 1611137024 | bytes 3145728 | tf_op jit(solution)/shard_map/dot_general | solution.py:74
  66.4 0.6 convolution_multiply_fusion
  67.0 1.1 %fusion.35 = f32[256,512]{1,0:T(8,128)S(1)} fusion(f32[256,512]{1,0:T(8,128)S(1)} %convolution_multiply_fusion, f32[512,512]{0,1:T(8,128)S(1)} %convolution_subtract_fusion), kind=kOutput, calls=%fused_computation.82 | convolution fusion | flops 805306368 | bytes 2097152 | tf_op jit(solution)/shard_map/dot_general | solution.py:78
  68.1 0.6 fusion.9
  69.0 8.4 %all_to_all.30 = f32[256,1,256]{2,1,0:T(1,128)S(1)} all-to-all(f32[256,1,256]{2,1,0:T(1,128)S(1)} %copy.50), channel_id=1, replica_groups=mesh['mem'=4,'lat'=8] {'mem'}, dimensions={0} | all-to-all | bytes 524288 | tf_op jit(solution)/shard_map/all_to_all | solution.py:126
  77.5 0.9 %reshape.77 = f32[64,2,512]{2,1,0:T(2,128)} reshape(f32[64,4,1,256]{3,1,0,2:T(4,128)S(1)} %copy.51) | data formatting | bytes 524288 | tf_op jit(solution)/shard_map/reshape | solution.py:127
  (60 shorter events, 5.9 us)
Async XLA Ops:
  0.0 17.5 %collective-permute-start = (f32[64,2,512]{2,1,0:T(2,128)}, f32[64,2,512]{2,1,0:T(2,128)S(1)}, u32[]{:S(2)}, u32[]{:S(2)}) collective-permute-start(f32[64,2,512]{2,1,0:T(2,128)} %param.9), channel_id=1, source_target_pairs={{0,1},{1,2},{2,3},{3,4},{4,5},{5,6},{6,7},{8,9},{9,10},{10,11},{11... | collective-permute-start | bytes 786440 | tf_op jit(solution)/shard_map/ppermute | solution.py:34
  4.9 12.6 %collective-permute-start.1 = (f32[64,2,512]{2,1,0:T(2,128)}, f32[64,2,512]{2,1,0:T(2,128)S(1)}, u32[]{:S(2)}, u32[]{:S(2)}) collective-permute-start(f32[64,2,512]{2,1,0:T(2,128)} %param.9), channel_id=1, source_target_pairs={{1,0},{2,1},{3,2},{4,3},{5,4},{6,5},{7,6},{9,8},{10,9},{11,10},{12... | collective-permute-start | bytes 786440 | tf_op jit(solution)/shard_map/ppermute | solution.py:37
  6.2 6.7 %copy-start.4 = (s32[1,4,4]{2,1,0:T(4,128)S(1)}, s32[1,4,4]{2,1,0:T(4,128)}, u32[]{:S(2)}) copy-start(s32[1,4,4]{2,1,0:T(4,128)} %param.12) | copy-start | bytes 196
  7.0 6.0 %copy-start.3 = (s32[1,4,512]{2,1,0:T(4,128)S(1)}, s32[1,4,512]{2,1,0:T(4,128)}, u32[]{:S(2)}) copy-start(s32[1,4,512]{2,1,0:T(4,128)} %param.13) | copy-start | bytes 24580
  7.0 9.5 %collective-permute-start.2 = (f32[2,1,512]{2,1,0:T(1,128)S(1)}, f32[2,1,512]{2,1,0:T(1,128)S(1)}, u32[]{:S(2)}, u32[]{:S(2)}) collective-permute-start(f32[2,1,512]{2,1,0:T(1,128)S(1)} %get-tuple-element.18), channel_id=1, source_target_pairs={{0,1},{1,2},{2,3},{3,4},{4,5},{5,6},{6,7},{8,9},{9,10},{10,11},{11... | collective-permute-start | bytes 12296 | tf_op jit(solution)/shard_map/ppermute | solution.py:34
  11.6 5.9 %collective-permute-start.3 = (f32[2,1,512]{2,1,0:T(1,128)S(1)}, f32[2,1,512]{2,1,0:T(1,128)S(1)}, u32[]{:S(2)}, u32[]{:S(2)}) collective-permute-start(f32[2,1,512]{2,1,0:T(1,128)S(1)} %get-tuple-element.19), channel_id=1, source_target_pairs={{1,0},{2,1},{3,2},{4,3},{5,4},{6,5},{7,6},{9,8},{10,9},{11,10},{12... | collective-permute-start | bytes 12296 | tf_op jit(solution)/shard_map/ppermute | solution.py:37
  13.0 4.4 %copy-start.2 = (f32[2,512]{1,0:T(2,128)S(1)}, f32[2,512]{1,0:T(2,128)}, u32[]{:S(2)}) copy-start(f32[2,512]{1,0:T(2,128)} %param.11) | copy-start | bytes 12292
  13.1 4.4 %copy-start.1 = (f32[2,512]{1,0:T(2,128)S(1)}, f32[2,512]{1,0:T(2,128)}, u32[]{:S(2)}) copy-start(f32[2,512]{1,0:T(2,128)} %param.10) | copy-start | bytes 12292
  18.8 1.0 %copy-start = (f32[64,2,512]{2,1,0:T(2,128)S(1)}, f32[64,2,512]{2,1,0:T(2,128)}, u32[]{:S(2)}) copy-start(f32[64,2,512]{2,1,0:T(2,128)} %param.9) | copy-start | bytes 786436
  27.4 14.6 %all-to-all-start = ((f32[64,4,512]{2,0,1:T(8,128)}), f32[64,4,512]{2,0,1:T(8,128)S(1)}, u32[]{:S(2)}, u32[]{:S(2)}) async-start(f32[64,4,512]{2,0,1:T(8,128)} %copy.45), calls=%async_computation | async-start | bytes 1048576 | tf_op jit(solution)/shard_map/all_to_all | solution.py:110
  31.3 2.1 %collective-permute-start.4 = (f32[64,1,256]{2,0,1:T(8,128)S(1)}, f32[64,1,256]{2,0,1:T(8,128)S(1)}, u32[]{:S(2)}, u32[]{:S(2)}) collective-permute-start(f32[64,1,256]{2,0,1:T(8,128)S(1)} %copy.57), channel_id=1, source_target_pairs={{0,8},{8,0},{16,24},{24,16},{1,9},{9,1},{17,25},{25,17},{2,10},{10... | collective-permute-start | bytes 196616 | tf_op jit(solution)/shard_map/ppermute | solution.py:24
  31.7 10.0 %collective-permute-start.5 = (f32[64,1,256]{2,0,1:T(8,128)S(1)}, f32[64,1,256]{2,0,1:T(8,128)S(1)}, u32[]{:S(2)}, u32[]{:S(2)}) collective-permute-start(f32[64,1,256]{2,0,1:T(8,128)S(1)} %copy.58), channel_id=1, source_target_pairs={{0,16},{8,24},{16,0},{24,8},{1,17},{9,25},{17,1},{25,9},{2,18},{10... | collective-permute-start | bytes 196616 | tf_op jit(solution)/shard_map/ppermute | solution.py:24
  33.3 8.6 %collective-permute-start.6 = (f32[64,1,256]{2,0,1:T(8,128)S(1)}, f32[64,1,256]{2,0,1:T(8,128)S(1)}, u32[]{:S(2)}, u32[]{:S(2)}) collective-permute-start(f32[64,1,256]{2,0,1:T(8,128)S(1)} %copy.59), channel_id=1, source_target_pairs={{0,24},{8,16},{16,8},{24,0},{1,25},{9,17},{17,9},{25,1},{2,26},{10... | collective-permute-start | bytes 196616 | tf_op jit(solution)/shard_map/ppermute | solution.py:24
  42.0 0.7 copy-start.5
  42.7 0.7 copy-start.6
